TPU v7x, 512 devices: a whole 4x4x16 slice. The times are simulated.
512 devices in a mesh: slot: 16 (over z_lo, x), row: 32 (over y, z_hi, core).
Axes of the slice: x: 4, y: 4, z: 16 (z_hi: 4, z_lo: 4; z = z_hi * 4 + z_lo), core: 2. Of those that a mesh axis runs over, the one named last changes fastest.
Arguments:
- drift: bfloat16 [2048, 2048], P(('slot', 'row')), may hold values from -1 to 1, as said below
- ctrl_blocks: bfloat16 [16, 128, 128], replicated, may hold values from -0.125 to 0.125
- blk_pos: int32 [16, 2], replicated, may hold values from 0 to 15
- amps: float32 [16, 16], P('slot'), may hold values from -4 to 4
- init_states: float32 [2, 512, 2048], P(None, 'row'), may hold values from -6 to 6
- targets: float32 [2, 512, 2048], P(None, 'row'), may hold values from -50 to 50
Outputs:
- states: float32 [16, 2, 512, 2048], P('slot', None, 'row')
- grads: float32 [16, 16], P('slot')
Inputs may be any that keep to these rules, and one draw needn't show every extreme that they name: drift is symmetric.
All inputs are finite; a program needn't handle non-finite values.
Results may differ from a plain program's by a relative error of at most 0.038.
Values may be sent and summed in bfloat16 or wider, within the bound.
No kernel may reach another device: no remote copies, remote signals or barrier semaphores. Data moves between devices by JAX's collectives and lax.ppermute only.
A program may use at most 64 MiB of HBM per device.

v0:
```python
import jax
import jax.numpy as jnp
from jax import lax
from jax.sharding import PartitionSpec as P

TAYLOR = 4


def passed_along(value, axis, steps):
    count = lax.axis_size(axis)
    initial, last = (max(0, -steps), min(count, count - steps))
    return lax.ppermute(value, axis, [(source, source + steps) for source in range(initial, last)])


def apply_hamiltonian(
    rounded, drift_full, ctrl_blocks, row_pick, col_pick, row_hot, col_hot, amps_row
):
    halves, columns, extent = rounded.shape
    block_size = ctrl_blocks.shape[1]
    flat_rows = rounded.reshape(halves * columns, extent)
    drift_part = jnp.dot(flat_rows, drift_full, preferred_element_type=jnp.float32)
    tile_rows = flat_rows.reshape(halves * columns, extent // block_size, block_size)
    from_col = jnp.take(tile_rows, col_pick, axis=1)
    from_row = jnp.take(tile_rows, row_pick, axis=1)
    upper_part = (
        jnp.einsum("mkb,kab->mka", from_col, ctrl_blocks, preferred_element_type=jnp.float32)
        * amps_row[None, :, None]
    )
    lower_part = (
        jnp.einsum("mka,kab->mkb", from_row, ctrl_blocks, preferred_element_type=jnp.float32)
        * amps_row[None, :, None]
    )
    placed = jnp.einsum("mka,kn->mna", upper_part, row_hot, precision=lax.Precision.HIGHEST)
    placed = placed + jnp.einsum(
        "mkb,kn->mnb", lower_part, col_hot, precision=lax.Precision.HIGHEST
    )
    summed = drift_part + placed.reshape(halves * columns, extent)
    return summed.reshape(halves, columns, extent)


def propagate(state, forward, apply_fn):
    summed = state
    series_term = state
    for degree in range(1, TAYLOR + 1):
        applied = apply_fn(series_term.astype(jnp.bfloat16))
        if forward:
            turned = jnp.stack([applied[1], -applied[0]])
        else:
            turned = jnp.stack([-applied[1], applied[0]])
        series_term = turned * (1.0 / degree)
        summed = summed + series_term
    return summed


def control_grads(state, adjoint, ctrl_blocks, row_pick, col_pick, scale):
    halves, columns, extent = state.shape
    block_size = ctrl_blocks.shape[1]
    shape_tiles = (halves * columns, extent // block_size, block_size)
    source = jnp.stack([state[1].astype(jnp.bfloat16), -state[0].astype(jnp.bfloat16)]).reshape(
        shape_tiles
    )
    weights = adjoint.astype(jnp.bfloat16).reshape(shape_tiles)
    upper_part = jnp.einsum(
        "mkb,kab->mka",
        jnp.take(source, col_pick, axis=1),
        ctrl_blocks,
        preferred_element_type=jnp.float32,
    )
    lower_part = jnp.einsum(
        "mka,kab->mkb",
        jnp.take(source, row_pick, axis=1),
        ctrl_blocks,
        preferred_element_type=jnp.float32,
    )
    inner_sum = jnp.sum(
        jnp.take(weights, row_pick, axis=1).astype(jnp.float32) * upper_part, axis=(0, 2)
    )
    inner_sum = inner_sum + jnp.sum(
        jnp.take(weights, col_pick, axis=1).astype(jnp.float32) * lower_part, axis=(0, 2)
    )
    return inner_sum * scale


def blank(values):
    return jnp.zeros_like(values)


def shards(drift, ctrl_blocks, blk_pos, amps, init_states, targets):
    drift_full = lax.all_gather(drift, ("slot", "row"), axis=0, tiled=True)
    block_count = drift_full.shape[0] // ctrl_blocks.shape[1]
    row_pick = blk_pos[:, 0]
    col_pick = blk_pos[:, 1]
    positions = lax.broadcasted_iota(jnp.int32, (ctrl_blocks.shape[0], block_count), 1)
    row_hot = (positions == row_pick[:, None]).astype(jnp.float32)
    col_hot = (positions == col_pick[:, None]).astype(jnp.float32)
    amps_row = amps[0]

    def apply_fn(rounded):
        return apply_hamiltonian(
            rounded, drift_full, ctrl_blocks, row_pick, col_pick, row_hot, col_hot, amps_row
        )

    def forward_map(values):
        return propagate(values, True, apply_fn)

    def adjoint_map(values):
        return propagate(values, False, apply_fn)

    slot_index = lax.axis_index("slot")
    slot_count = lax.axis_size("slot")
    last_slot = slot_count - 1
    columns = init_states.shape[1]
    extent = init_states.shape[2]
    piece_count = 1
    width = columns // piece_count

    def split_cols(values):
        return values.reshape(2, piece_count, width, extent).transpose(1, 0, 2, 3)

    def join_cols(pieces):
        return pieces.transpose(1, 0, 2, 3).reshape(2, columns, extent)

    init_pieces = split_cols(init_states)
    target_pieces = split_cols(targets)
    tick_count = slot_count + piece_count - 1
    empty_all = jnp.zeros_like(init_pieces)
    empty_one = jnp.zeros_like(init_pieces[0])

    def forward_update(step, stored, arrived):
        order = step - slot_index
        active = (order >= 0) & (order < piece_count)
        place = jnp.clip(order, 0, piece_count - 1)
        start_piece = lax.dynamic_index_in_dim(init_pieces, place, 0, keepdims=False)
        source = jnp.where(slot_index == 0, start_piece, arrived)
        result = lax.cond(active, forward_map, blank, source)
        updated = lax.dynamic_update_index_in_dim(stored, result, place, 0)
        stored = jnp.where(active, updated, stored)
        return (stored, result)

    def adjoint_update(step, stored, returned):
        order = step - (last_slot - slot_index)
        active = (order >= 0) & (order < piece_count)
        place = jnp.clip(order, 0, piece_count - 1)
        target_piece = lax.dynamic_index_in_dim(target_pieces, place, 0, keepdims=False)
        own = jnp.where(slot_index == last_slot, target_piece, returned)
        updated = lax.dynamic_update_index_in_dim(stored, own, place, 0)
        stored = jnp.where(active, updated, stored)
        outgoing = lax.cond(active & (slot_index > 0), adjoint_map, blank, own)
        return (stored, outgoing)

    def joint_tick(step, carry):
        fwd_stored, fwd_out, adj_stored, adj_out = carry
        arrived = passed_along(fwd_out.astype(jnp.bfloat16), "slot", 1).astype(fwd_out.dtype)
        returned = passed_along(adj_out.astype(jnp.bfloat16), "slot", -1).astype(adj_out.dtype)
        fwd_stored, fwd_out = forward_update(step, fwd_stored, arrived)
        adj_stored, adj_out = adjoint_update(step, adj_stored, returned)
        return (fwd_stored, fwd_out, adj_stored, adj_out)

    fwd_stored, _, adj_stored, _ = lax.fori_loop(
        0, tick_count, joint_tick, (empty_all, empty_one, empty_all, empty_one)
    )
    fwd_state = join_cols(fwd_stored)
    adj_mine = join_cols(adj_stored)
    scale = 1.0 / (columns * lax.axis_size("row"))
    partial_grads = control_grads(fwd_state, adj_mine, ctrl_blocks, row_pick, col_pick, scale)
    grads = lax.psum(partial_grads[None, :], "row")
    return (fwd_state[None], grads)


def solution(mesh):
    in_specs = (
        P(("slot", "row"), None),
        P(),
        P(),
        P("slot", None),
        P(None, "row", None),
        P(None, "row", None),
    )
    out_specs = (P("slot", None, "row", None), P("slot", None))
    return jax.shard_map(shards, mesh=mesh, in_specs=in_specs, out_specs=out_specs, check_vma=False)
```

profile of v0, /device:TPU:103, one launch (start us, length us, event | category | flops | bytes accessed | tf_op | source)
XLA Modules:
  0.0 1654.7 jit_solution(1172429229301434716)
XLA Ops:
  11.2 817.7 %all-gather.3.cloned.1.call-done = bf16[512,4,2048]{2,1,0:T(4,128)(2,1)} async-done(((bf16[1,4,2048]{2,1,0:T(4,128)(2,1)}), bf16[512,4,2048]{2,1,0:T(4,128)(2,1)}) %all-gather.3.cloned.1.call-update) | async-done | bytes 8388624 | tf_op jit(solution)/shard_map/all_gather | solution.py:89
  828.9 12.5 reshape.382
  842.2 692.2 %while.23 = (s32[]{:T(128)}, f32[1,2,16,2048]{3,2,1,0:T(8,128)S(1)}, f32[2,16,2048]{2,1,0:T(8,128)}, bf16[1,2,16,2048]{3,2,1,0:T(8,128)(2,1)S(1)}, bf16[2,16,204...) while((s32[]{:T(128)}, ...), condition=%wide.region_5.7_spmd.clone.clone.clone, body=%wide.region_0.6_spmd.clone.clone.clone.sunk | while | flops 2623804928 | bytes 120887232 | solution.py:159
  844.5 4.0 collective-permute-start.1
  848.6 2.2 collective-permute-done.1
  851.7 32.8 %conditional.11 = (bf16[2,16,2048]{2,1,0:T(8,128)(2,1)}) conditional(s32[]{:T(128)} %convert_element_type.218, () %tuple.106, (f32[2,16,2048]{2,1,0:T(8,128)S(1)}, bf16[2048,2048]{1,0:T(8,128)(2,1)}, s32[16]{0:T(128)S(1)}, bf16[16,128,128]{2,1,0:T(8,128)(2,1)S(1)}, f32[1,16]{1,0:T(1,128)S(1)}, /*index=5*/f32[16,16]{0,1:T(8,128)S(1)}, ...), branch_computations={%region_3.4_spmd, %region_4.5_spmd} | conditional | flops 1311639808 | bytes 58082984 | solution.py:148
  854.8 4.9 convolution_add_fusion.11
  862.8 4.9 convolution_add_fusion.10
  870.8 4.9 convolution_add_fusion.9
  878.8 4.9 convolution_add_fusion.8
  886.8 4.0 collective-permute-start.1
  890.8 2.2 collective-permute-done.1
  895.6 1.3 collective-permute-start
  896.9 36.4 %collective-permute-start.1 = (bf16[2,16,2048]{2,1,0:T(8,128)(2,1)}, bf16[2,16,2048]{2,1,0:T(8,128)(2,1)S(1)}, u32[]{:S(2)}, u32[]{:S(2)}) collective-permute-start(bf16[2,16,2048]{2,1,0:T(8,128)(2,1)} %get-tuple-element.768), channel_id=1, source_target_pairs={{32,0},{64,32},{96,64},{128,96},{160,128},{192,160},{224,192},{256... | collective-permute-start | bytes 393224 | tf_op jit(solution)/shard_map/while/body/eval_jaxpr/ppermute | solution.py:12
  933.4 2.2 collective-permute-done.1
  939.5 4.3 collective-permute-start.1
  943.9 3.2 collective-permute-done.1
  949.6 1.3 collective-permute-start
  950.9 35.1 %collective-permute-start.1 = (bf16[2,16,2048]{2,1,0:T(8,128)(2,1)}, bf16[2,16,2048]{2,1,0:T(8,128)(2,1)S(1)}, u32[]{:S(2)}, u32[]{:S(2)}) collective-permute-start(bf16[2,16,2048]{2,1,0:T(8,128)(2,1)} %get-tuple-element.768), channel_id=1, source_target_pairs={{32,0},{64,32},{96,64},{128,96},{160,128},{192,160},{224,192},{256... | collective-permute-start | bytes 393224 | tf_op jit(solution)/shard_map/while/body/eval_jaxpr/ppermute | solution.py:12
  986.1 2.2 collective-permute-done.1
  992.2 4.6 collective-permute-start.1
  996.9 2.2 collective-permute-done.1
  1003.0 35.8 %collective-permute-start.1 = (bf16[2,16,2048]{2,1,0:T(8,128)(2,1)}, bf16[2,16,2048]{2,1,0:T(8,128)(2,1)S(1)}, u32[]{:S(2)}, u32[]{:S(2)}) collective-permute-start(bf16[2,16,2048]{2,1,0:T(8,128)(2,1)} %get-tuple-element.768), channel_id=1, source_target_pairs={{32,0},{64,32},{96,64},{128,96},{160,128},{192,160},{224,192},{256... | collective-permute-start | bytes 393224 | tf_op jit(solution)/shard_map/while/body/eval_jaxpr/ppermute | solution.py:12
  1038.9 2.2 collective-permute-done.1
  1044.9 6.8 collective-permute-start.1
  1051.8 2.2 collective-permute-done.1
  1057.9 37.8 %collective-permute-start.1 = (bf16[2,16,2048]{2,1,0:T(8,128)(2,1)}, bf16[2,16,2048]{2,1,0:T(8,128)(2,1)S(1)}, u32[]{:S(2)}, u32[]{:S(2)}) collective-permute-start(bf16[2,16,2048]{2,1,0:T(8,128)(2,1)} %get-tuple-element.768), channel_id=1, source_target_pairs={{32,0},{64,32},{96,64},{128,96},{160,128},{192,160},{224,192},{256... | collective-permute-start | bytes 393224 | tf_op jit(solution)/shard_map/while/body/eval_jaxpr/ppermute | solution.py:12
  1095.8 2.2 collective-permute-done.1
  1101.9 6.4 collective-permute-start.1
  1108.3 2.2 collective-permute-done.1
  1114.4 34.0 %collective-permute-start.1 = (bf16[2,16,2048]{2,1,0:T(8,128)(2,1)}, bf16[2,16,2048]{2,1,0:T(8,128)(2,1)S(1)}, u32[]{:S(2)}, u32[]{:S(2)}) collective-permute-start(bf16[2,16,2048]{2,1,0:T(8,128)(2,1)} %get-tuple-element.768), channel_id=1, source_target_pairs={{32,0},{64,32},{96,64},{128,96},{160,128},{192,160},{224,192},{256... | collective-permute-start | bytes 393224 | tf_op jit(solution)/shard_map/while/body/eval_jaxpr/ppermute | solution.py:12
  1148.5 2.2 collective-permute-done.1
  1154.6 6.4 collective-permute-start.1
  1161.1 2.2 collective-permute-done.1
  1167.2 34.0 %collective-permute-start.1 = (bf16[2,16,2048]{2,1,0:T(8,128)(2,1)}, bf16[2,16,2048]{2,1,0:T(8,128)(2,1)S(1)}, u32[]{:S(2)}, u32[]{:S(2)}) collective-permute-start(bf16[2,16,2048]{2,1,0:T(8,128)(2,1)} %get-tuple-element.768), channel_id=1, source_target_pairs={{32,0},{64,32},{96,64},{128,96},{160,128},{192,160},{224,192},{256... | collective-permute-start | bytes 393224 | tf_op jit(solution)/shard_map/while/body/eval_jaxpr/ppermute | solution.py:12
  1201.2 2.2 collective-permute-done.1
  1207.3 6.4 collective-permute-start.1
  1213.8 2.2 collective-permute-done.1
  1219.9 34.0 %collective-permute-start.1 = (bf16[2,16,2048]{2,1,0:T(8,128)(2,1)}, bf16[2,16,2048]{2,1,0:T(8,128)(2,1)S(1)}, u32[]{:S(2)}, u32[]{:S(2)}) collective-permute-start(bf16[2,16,2048]{2,1,0:T(8,128)(2,1)} %get-tuple-element.768), channel_id=1, source_target_pairs={{32,0},{64,32},{96,64},{128,96},{160,128},{192,160},{224,192},{256... | collective-permute-start | bytes 393224 | tf_op jit(solution)/shard_map/while/body/eval_jaxpr/ppermute | solution.py:12
  1253.9 2.2 collective-permute-done.1
  1260.0 237.5 %collective-permute-start.1 = (bf16[2,16,2048]{2,1,0:T(8,128)(2,1)}, bf16[2,16,2048]{2,1,0:T(8,128)(2,1)S(1)}, u32[]{:S(2)}, u32[]{:S(2)}) collective-permute-start(bf16[2,16,2048]{2,1,0:T(8,128)(2,1)} %get-tuple-element.768), channel_id=1, source_target_pairs={{32,0},{64,32},{96,64},{128,96},{160,128},{192,160},{224,192},{256... | collective-permute-start | bytes 393224 | tf_op jit(solution)/shard_map/while/body/eval_jaxpr/ppermute | solution.py:12
  1497.6 2.2 collective-permute-done.1
  1499.9 33.8 %conditional.10 = (f32[2,16,2048]{2,1,0:T(8,128)}, f32[1,2,16,2048]{3,2,1,0:T(8,128)S(1)}) conditional(s32[]{:T(128)} %convert_element_type.215, () %tuple.104, (pred[]{:T(512)}, f32[1,2,16,2048]{3,2,1,0:T(8,128)S(1)}, f32[2,16,2048]{2,1,0:T(8,128)S(1)}, bf16[2048,2048]{1,0:T(8,128)(2,1)}, s32[16]{0:T(128)S(1)}, ...), branch_computations={%region_1.1_spmd, %region_2.3_spmd} | conditional | flops 1311639808 | bytes 59262640 | solution.py:135
  1503.0 4.9 convolution_add_fusion.3
  1511.0 4.9 convolution_add_fusion.2
  1519.0 4.9 convolution_add_fusion.1
  1527.0 4.9 convolution_add_fusion
  1538.5 109.4 %psum.7 = f32[1,16]{1,0:T(1,128)} all-reduce(f32[1,16]{1,0:T(1,128)S(1)} %multiply_bitcast_fusion), channel_id=1, replica_groups=mesh['slot'=16,'row'=32] {'row'}, use_global_device_ids=true, to_apply=%region_8.10 | all-reduce | flops 16 | bytes 128 | tf_op jit(solution)/shard_map/psum | solution.py:166
  (313 shorter events, 114.0 us)
Async XLA Ops:
  7.2 821.8 %all-gather.3.cloned.1.call-start = ((), (), s32[]{:S(2)}) async-start(), calls=%async_computation | async-start | bytes 8404992 | tf_op jit(solution)/shard_map/all_gather | solution.py:89
  11.2 831.0 %copy-start = (bf16[16,128,128]{2,1,0:T(8,128)(2,1)S(1)}, bf16[16,128,128]{2,1,0:T(8,128)(2,1)}, u32[]{:S(2)}) copy-start(bf16[16,128,128]{2,1,0:T(8,128)(2,1)} %param.15) | copy-start | bytes 1572868
  11.2 831.0 %copy-start.1 = (f32[2,16,2048]{2,1,0:T(8,128)S(1)}, f32[2,16,2048]{2,1,0:T(8,128)}, u32[]{:S(2)}) copy-start(f32[2,16,2048]{2,1,0:T(8,128)} %param.18) | copy-start | bytes 786436
  11.2 831.0 %copy-start.3 = (f32[2,16,2048]{2,1,0:T(8,128)S(1)}, f32[2,16,2048]{2,1,0:T(8,128)}, u32[]{:S(2)}) copy-start(f32[2,16,2048]{2,1,0:T(8,128)} %param.19) | copy-start | bytes 786436
  11.2 831.0 %copy-start.4 = (f32[1,16]{1,0:T(1,128)S(1)}, f32[1,16]{1,0:T(1,128)}, u32[]{:S(2)}) copy-start(f32[1,16]{1,0:T(1,128)} %param.17) | copy-start | bytes 196
  842.2 695.3 %copy-start.5 = (pred[16]{0:T(512)(128)(4,1)S(1)}, pred[16]{0:T(512)(128)(4,1)}, u32[]{:S(2)}) copy-start(pred[16]{0:T(512)(128)(4,1)} %get-tuple-element.588) | copy-start | bytes 52
  842.2 695.3 %copy-start.6 = (pred[16]{0:T(512)(128)(4,1)S(1)}, pred[16]{0:T(512)(128)(4,1)}, u32[]{:S(2)}) copy-start(pred[16]{0:T(512)(128)(4,1)} %get-tuple-element.620) | copy-start | bytes 52
  843.2 7.6 collective-permute-start
  844.5 6.2 collective-permute-start.1
  885.5 7.6 collective-permute-start
  886.8 6.2 collective-permute-start.1
  895.6 40.1 %collective-permute-start = (bf16[2,16,2048]{2,1,0:T(8,128)(2,1)S(1)}, bf16[2,16,2048]{2,1,0:T(8,128)(2,1)S(1)}, u32[]{:S(2)}, u32[]{:S(2)}) collective-permute-start(bf16[2,16,2048]{2,1,0:T(8,128)(2,1)S(1)} %convert_element_type.216), channel_id=1, source_target_pairs={{0,32},{32,64},{64,96},{96,128},{128,160},{160,192},{192,224},{224... | collective-permute-start | bytes 393224 | tf_op jit(solution)/shard_map/while/body/eval_jaxpr/ppermute | solution.py:12
  896.9 38.7 %collective-permute-start.1 = (bf16[2,16,2048]{2,1,0:T(8,128)(2,1)}, bf16[2,16,2048]{2,1,0:T(8,128)(2,1)S(1)}, u32[]{:S(2)}, u32[]{:S(2)}) collective-permute-start(bf16[2,16,2048]{2,1,0:T(8,128)(2,1)} %get-tuple-element.768), channel_id=1, source_target_pairs={{32,0},{64,32},{96,64},{128,96},{160,128},{192,160},{224,192},{256... | collective-permute-start | bytes 393224 | tf_op jit(solution)/shard_map/while/body/eval_jaxpr/ppermute | solution.py:12
  938.2 8.9 collective-permute-start
  939.5 7.5 collective-permute-start.1
  949.6 38.8 %collective-permute-start = (bf16[2,16,2048]{2,1,0:T(8,128)(2,1)S(1)}, bf16[2,16,2048]{2,1,0:T(8,128)(2,1)S(1)}, u32[]{:S(2)}, u32[]{:S(2)}) collective-permute-start(bf16[2,16,2048]{2,1,0:T(8,128)(2,1)S(1)} %convert_element_type.216), channel_id=1, source_target_pairs={{0,32},{32,64},{64,96},{96,128},{128,160},{160,192},{192,224},{224... | collective-permute-start | bytes 393224 | tf_op jit(solution)/shard_map/while/body/eval_jaxpr/ppermute | solution.py:12
  950.9 37.4 %collective-permute-start.1 = (bf16[2,16,2048]{2,1,0:T(8,128)(2,1)}, bf16[2,16,2048]{2,1,0:T(8,128)(2,1)S(1)}, u32[]{:S(2)}, u32[]{:S(2)}) collective-permute-start(bf16[2,16,2048]{2,1,0:T(8,128)(2,1)} %get-tuple-element.768), channel_id=1, source_target_pairs={{32,0},{64,32},{96,64},{128,96},{160,128},{192,160},{224,192},{256... | collective-permute-start | bytes 393224 | tf_op jit(solution)/shard_map/while/body/eval_jaxpr/ppermute | solution.py:12
  990.9 8.2 collective-permute-start
  992.2 6.9 collective-permute-start.1
  1001.7 39.4 %collective-permute-start = (bf16[2,16,2048]{2,1,0:T(8,128)(2,1)S(1)}, bf16[2,16,2048]{2,1,0:T(8,128)(2,1)S(1)}, u32[]{:S(2)}, u32[]{:S(2)}) collective-permute-start(bf16[2,16,2048]{2,1,0:T(8,128)(2,1)S(1)} %convert_element_type.216), channel_id=1, source_target_pairs={{0,32},{32,64},{64,96},{96,128},{128,160},{160,192},{192,224},{224... | collective-permute-start | bytes 393224 | tf_op jit(solution)/shard_map/while/body/eval_jaxpr/ppermute | solution.py:12
  1003.0 38.1 %collective-permute-start.1 = (bf16[2,16,2048]{2,1,0:T(8,128)(2,1)}, bf16[2,16,2048]{2,1,0:T(8,128)(2,1)S(1)}, u32[]{:S(2)}, u32[]{:S(2)}) collective-permute-start(bf16[2,16,2048]{2,1,0:T(8,128)(2,1)} %get-tuple-element.768), channel_id=1, source_target_pairs={{32,0},{64,32},{96,64},{128,96},{160,128},{192,160},{224,192},{256... | collective-permute-start | bytes 393224 | tf_op jit(solution)/shard_map/while/body/eval_jaxpr/ppermute | solution.py:12
  1043.6 10.4 collective-permute-start
  1044.9 9.1 collective-permute-start.1
  1056.6 41.5 %collective-permute-start = (bf16[2,16,2048]{2,1,0:T(8,128)(2,1)S(1)}, bf16[2,16,2048]{2,1,0:T(8,128)(2,1)S(1)}, u32[]{:S(2)}, u32[]{:S(2)}) collective-permute-start(bf16[2,16,2048]{2,1,0:T(8,128)(2,1)S(1)} %convert_element_type.216), channel_id=1, source_target_pairs={{0,32},{32,64},{64,96},{96,128},{128,160},{160,192},{192,224},{224... | collective-permute-start | bytes 393224 | tf_op jit(solution)/shard_map/while/body/eval_jaxpr/ppermute | solution.py:12
  1057.9 40.1 %collective-permute-start.1 = (bf16[2,16,2048]{2,1,0:T(8,128)(2,1)}, bf16[2,16,2048]{2,1,0:T(8,128)(2,1)S(1)}, u32[]{:S(2)}, u32[]{:S(2)}) collective-permute-start(bf16[2,16,2048]{2,1,0:T(8,128)(2,1)} %get-tuple-element.768), channel_id=1, source_target_pairs={{32,0},{64,32},{96,64},{128,96},{160,128},{192,160},{224,192},{256... | collective-permute-start | bytes 393224 | tf_op jit(solution)/shard_map/while/body/eval_jaxpr/ppermute | solution.py:12
  1100.6 10.0 collective-permute-start
  1101.9 8.7 collective-permute-start.1
  1113.1 37.6 %collective-permute-start = (bf16[2,16,2048]{2,1,0:T(8,128)(2,1)S(1)}, bf16[2,16,2048]{2,1,0:T(8,128)(2,1)S(1)}, u32[]{:S(2)}, u32[]{:S(2)}) collective-permute-start(bf16[2,16,2048]{2,1,0:T(8,128)(2,1)S(1)} %convert_element_type.216), channel_id=1, source_target_pairs={{0,32},{32,64},{64,96},{96,128},{128,160},{160,192},{192,224},{224... | collective-permute-start | bytes 393224 | tf_op jit(solution)/shard_map/while/body/eval_jaxpr/ppermute | solution.py:12
  1114.4 36.3 %collective-permute-start.1 = (bf16[2,16,2048]{2,1,0:T(8,128)(2,1)}, bf16[2,16,2048]{2,1,0:T(8,128)(2,1)S(1)}, u32[]{:S(2)}, u32[]{:S(2)}) collective-permute-start(bf16[2,16,2048]{2,1,0:T(8,128)(2,1)} %get-tuple-element.768), channel_id=1, source_target_pairs={{32,0},{64,32},{96,64},{128,96},{160,128},{192,160},{224,192},{256... | collective-permute-start | bytes 393224 | tf_op jit(solution)/shard_map/while/body/eval_jaxpr/ppermute | solution.py:12
  1153.3 10.0 collective-permute-start
  1154.6 8.7 collective-permute-start.1
  1165.9 37.6 %collective-permute-start = (bf16[2,16,2048]{2,1,0:T(8,128)(2,1)S(1)}, bf16[2,16,2048]{2,1,0:T(8,128)(2,1)S(1)}, u32[]{:S(2)}, u32[]{:S(2)}) collective-permute-start(bf16[2,16,2048]{2,1,0:T(8,128)(2,1)S(1)} %convert_element_type.216), channel_id=1, source_target_pairs={{0,32},{32,64},{64,96},{96,128},{128,160},{160,192},{192,224},{224... | collective-permute-start | bytes 393224 | tf_op jit(solution)/shard_map/while/body/eval_jaxpr/ppermute | solution.py:12
  1167.2 36.3 %collective-permute-start.1 = (bf16[2,16,2048]{2,1,0:T(8,128)(2,1)}, bf16[2,16,2048]{2,1,0:T(8,128)(2,1)S(1)}, u32[]{:S(2)}, u32[]{:S(2)}) collective-permute-start(bf16[2,16,2048]{2,1,0:T(8,128)(2,1)} %get-tuple-element.768), channel_id=1, source_target_pairs={{32,0},{64,32},{96,64},{128,96},{160,128},{192,160},{224,192},{256... | collective-permute-start | bytes 393224 | tf_op jit(solution)/shard_map/while/body/eval_jaxpr/ppermute | solution.py:12
  1206.0 10.0 collective-permute-start
  1207.3 8.7 collective-permute-start.1
  1218.6 37.6 %collective-permute-start = (bf16[2,16,2048]{2,1,0:T(8,128)(2,1)S(1)}, bf16[2,16,2048]{2,1,0:T(8,128)(2,1)S(1)}, u32[]{:S(2)}, u32[]{:S(2)}) collective-permute-start(bf16[2,16,2048]{2,1,0:T(8,128)(2,1)S(1)} %convert_element_type.216), channel_id=1, source_target_pairs={{0,32},{32,64},{64,96},{96,128},{128,160},{160,192},{192,224},{224... | collective-permute-start | bytes 393224 | tf_op jit(solution)/shard_map/while/body/eval_jaxpr/ppermute | solution.py:12
  1219.9 36.3 %collective-permute-start.1 = (bf16[2,16,2048]{2,1,0:T(8,128)(2,1)}, bf16[2,16,2048]{2,1,0:T(8,128)(2,1)S(1)}, u32[]{:S(2)}, u32[]{:S(2)}) collective-permute-start(bf16[2,16,2048]{2,1,0:T(8,128)(2,1)} %get-tuple-element.768), channel_id=1, source_target_pairs={{32,0},{64,32},{96,64},{128,96},{160,128},{192,160},{224,192},{256... | collective-permute-start | bytes 393224 | tf_op jit(solution)/shard_map/while/body/eval_jaxpr/ppermute | solution.py:12
  1258.7 241.1 %collective-permute-start = (bf16[2,16,2048]{2,1,0:T(8,128)(2,1)S(1)}, bf16[2,16,2048]{2,1,0:T(8,128)(2,1)S(1)}, u32[]{:S(2)}, u32[]{:S(2)}) collective-permute-start(bf16[2,16,2048]{2,1,0:T(8,128)(2,1)S(1)} %convert_element_type.216), channel_id=1, source_target_pairs={{0,32},{32,64},{64,96},{96,128},{128,160},{160,192},{192,224},{224... | collective-permute-start | bytes 393224 | tf_op jit(solution)/shard_map/while/body/eval_jaxpr/ppermute | solution.py:12
  1260.0 239.7 %collective-permute-start.1 = (bf16[2,16,2048]{2,1,0:T(8,128)(2,1)}, bf16[2,16,2048]{2,1,0:T(8,128)(2,1)S(1)}, u32[]{:S(2)}, u32[]{:S(2)}) collective-permute-start(bf16[2,16,2048]{2,1,0:T(8,128)(2,1)} %get-tuple-element.768), channel_id=1, source_target_pairs={{32,0},{64,32},{96,64},{128,96},{160,128},{192,160},{224,192},{256... | collective-permute-start | bytes 393224 | tf_op jit(solution)/shard_map/while/body/eval_jaxpr/ppermute | solution.py:12
  1534.5 113.4 %copy-start.2 = (f32[1,2,16,2048]{3,2,1,0:T(8,128)}, f32[1,2,16,2048]{3,2,1,0:T(8,128)S(1)}, u32[]{:S(2)}) copy-start(f32[1,2,16,2048]{3,2,1,0:T(8,128)S(1)} %get-tuple-element.394) | copy-start | bytes 786436
Sparse Core Ops, SparseCore 0:
  10.2 818.6 all-gather.2
where the time goes:
time: 1660 us; the launch traced here: 1650 us
  waiting for transfers between devices  855 us (52%)
  starting transfers between devices  548 us (33%)
  blocking collectives  109 us (7%)
  matrix products  54.5 us (3%)
  local copies, waits for them, and re-layouts  48.5 us (3%)
  other arithmetic  22.7 us (1%)
    all_gather x1, waiting for transfers between devices, shards(): drift_full = lax.all_gather(drift, ('slot', 'row'), axis=0, tiled=True)  818 us
    ppermute x32, starting transfers between devices, passed_along(): lax.ppermute(value, axis, [(source, source + steps) for source in range(i...  548 us
    psum x1, blocking collectives, shards(): grads = lax.psum(partial_grads[None, :], 'row')  109 us
    dot_general x8, matrix products, apply_hamiltonian(): jnp.dot(flat_rows, drift_full, preferred_element_type=jnp.float32)  39.5 us
    ppermute x32, waiting for transfers between devices, passed_along(): lax.ppermute(value, axis, [(source, source + steps) for source in range(i...  36.2 us
  transfers between devices with their start and end apart: 33, of which 17 were waited for; matrix products, arithmetic and copies ran while one was open for 0% of the time, Pallas kernels for 0%

commit v1 on v0

--- a/solution.py
+++ b/solution.py
@@ -4,6 +4,15 @@
 from jax.sharding import PartitionSpec as P
 
 TAYLOR = 4
+pack_strings_now = lambda own_rows: jnp.concatenate(
+    lax.all_to_all(
+        jnp.stack(lax.axis_size(("slot", "row")) * [own_rows]),
+        concat_axis=0,
+        split_axis=0,
+        axis_name=("slot", "row"),
+    ),
+    axis=0,
+)
 
 
 def passed_along(value, axis, steps):
@@ -86,7 +95,7 @@
 
 
 def shards(drift, ctrl_blocks, blk_pos, amps, init_states, targets):
-    drift_full = lax.all_gather(drift, ("slot", "row"), axis=0, tiled=True)
+    drift_full = pack_strings_now(drift)
     block_count = drift_full.shape[0] // ctrl_blocks.shape[1]
     row_pick = blk_pos[:, 0]
     col_pick = blk_pos[:, 1]

time: 1660 us -> 1340 us (0.81)
  waiting for transfers between devices: 855 us -> 645 us
  starting transfers between devices: 548 us -> 423 us
    all_gather x1 -> x0, waiting for transfers between devices: 818 us -> none  [shards(): drift_full = lax.all_gather(drift, ('slot', 'row'), axis=0, tiled=True)]
    all_to_all x0 -> x1, waiting for transfers between devices: none -> 359 us  [lax.all_to_all(jnp.stack(lax.axis_size(('slot', 'row')) * [own_rows]), co...]
    ppermute x32, waiting for transfers between devices: 36.2 us -> 286 us  [passed_along(): lax.ppermute(value, axis, [(source, source + steps) for source in range(i...]
    ppermute x32, starting transfers between devices: 548 us -> 398 us  [passed_along(): lax.ppermute(value, axis, [(source, source + steps) for source in range(i...]
    all_to_all x0 -> x1, starting transfers between devices: none -> 25 us  [lax.all_to_all(jnp.stack(lax.axis_size(('slot', 'row')) * [own_rows]), co...]
  transfers between devices with their start and end apart: 33 -> 33, of which waited for: 17 -> 17; matrix products, arithmetic and copies ran while one was open for 0% -> 2% of each run, Pallas kernels for 0% -> 0%
where the time goes in v1:
time: 1340 us
  waiting for transfers between devices  645 us (48%)
  starting transfers between devices  423 us (32%)
  blocking collectives  110 us (8%)
  matrix products  65 us (5%)
  local copies, waits for them, and re-layouts  56.5 us (4%)
  other arithmetic  34.9 us (3%)
    ppermute x32, starting transfers between devices, passed_along(): lax.ppermute(value, axis, [(source, source + steps) for source in range(i...  398 us
    all_to_all x1, waiting for transfers between devices, lax.all_to_all(jnp.stack(lax.axis_size(('slot', 'row')) * [own_rows]), co...  359 us
    ppermute x32, waiting for transfers between devices, passed_along(): lax.ppermute(value, axis, [(source, source + steps) for source in range(i...  286 us
    psum x1, blocking collectives, shards(): grads = lax.psum(partial_grads[None, :], 'row')  110 us
    dot_general x8, matrix products, apply_hamiltonian(): jnp.dot(flat_rows, drift_full, preferred_element_type=jnp.float32)  39.5 us
  transfers between devices with their start and end apart: 33, of which 17 were waited for; matrix products, arithmetic and copies ran while one was open for 2% of the time, Pallas kernels for 0%

profile of v1, /device:TPU:103, one launch (start us, length us, event | category | flops | bytes accessed | tf_op | source)
XLA Modules:
  0.0 1338.0 jit_solution(14209233948235574569)
XLA Ops:
  0.6 8.3 stack.20
  8.9 25.0 %all-to-all-start = ((bf16[512,4,2048]{2,1,0:T(4,128)(2,1)}), bf16[512,4,2048]{2,1,0:T(4,128)(2,1)}, u32[]{:S(2)}, u32[]{:S(2)}) async-start(bf16[512,4,2048]{2,1,0:T(4,128)(2,1)} %stack.20), calls=%async_computation | async-start | bytes 16777216 | tf_op jit(solution)/shard_map/all_to_all | solution.py:8
  36.3 359.3 %all-to-all-done = bf16[512,4,2048]{2,1,0:T(4,128)(2,1)} async-done(((bf16[512,4,2048]{2,1,0:T(4,128)(2,1)}), bf16[512,4,2048]{2,1,0:T(4,128)(2,1)}, u32[]{:S(2)}, u32[]{:S(2)}) %all-to-all-start) | async-done | bytes 8388640 | tf_op jit(solution)/shard_map/all_to_all | solution.py:8
  395.6 12.5 reshape.205
  408.9 814.6 %while.23 = (s32[]{:T(128)}, f32[1,2,16,2048]{3,2,1,0:T(8,128)S(1)}, f32[2,16,2048]{2,1,0:T(8,128)}, bf16[1,2,16,2048]{3,2,1,0:T(8,128)(2,1)S(1)}, bf16[2,16,204...) while((s32[]{:T(128)}, ...), condition=%wide.region_5.7_spmd.clone.clone.clone, body=%wide.region_0.6_spmd.clone.clone.clone.sunk | while | flops 2623804928 | bytes 120887232 | solution.py:168
  409.1 2.2 collective-permute-start.1
  414.3 4.8 collective-permute-done
  420.0 39.3 %conditional.11 = (bf16[2,16,2048]{2,1,0:T(8,128)(2,1)}) conditional(s32[]{:T(128)} %convert_element_type.218, () %tuple.106, (f32[2,16,2048]{2,1,0:T(8,128)S(1)}, bf16[2048,2048]{1,0:T(8,128)(2,1)}, s32[16]{0:T(128)}, bf16[16,128,128]{2,1,0:T(8,128)(2,1)S(1)}, f32[1,16]{1,0:T(1,128)}, /*index=5*/f32[16,16]{0,1:T(8,128)S(1)}, s32[16]{0:T(128)}, ...), branch_computations={%region_3.4_spmd, %region_4.5_spmd} | conditional | flops 1311639808 | bytes 58082984 | solution.py:157
  425.6 4.9 convolution_add_fusion.11
  434.9 4.9 convolution_add_fusion.10
  444.2 4.9 convolution_add_fusion.9
  453.6 4.9 convolution_add_fusion.8
  463.6 3.7 collective-permute-done
  468.8 40.1 %collective-permute-start.1 = (bf16[2,16,2048]{2,1,0:T(8,128)(2,1)}, bf16[2,16,2048]{2,1,0:T(8,128)(2,1)S(1)}, u32[]{:S(2)}, u32[]{:S(2)}) collective-permute-start(bf16[2,16,2048]{2,1,0:T(8,128)(2,1)} %get-tuple-element.768), channel_id=1, source_target_pairs={{32,0},{64,32},{96,64},{128,96},{160,128},{192,160},{224,192},{256... | collective-permute-start | bytes 393224 | tf_op jit(solution)/shard_map/while/body/eval_jaxpr/ppermute | solution.py:21
  511.9 3.7 collective-permute-done
  517.1 1.9 collective-permute-start.1
  522.1 40.4 %collective-permute-done = bf16[2,16,2048]{2,1,0:T(8,128)(2,1)S(1)} collective-permute-done((bf16[2,16,2048]{2,1,0:T(8,128)(2,1)S(1)}, bf16[2,16,2048]{2,1,0:T(8,128)(2,1)S(1)}, u32[]{:S(2)}, u32[]{:S(2)}) %collective-permute-start) | collective-permute-done | bytes 131104 | tf_op jit(solution)/shard_map/while/body/eval_jaxpr/ppermute | solution.py:21
  564.1 3.4 collective-permute-start.1
  570.4 3.7 collective-permute-done
  575.6 38.7 %collective-permute-start.1 = (bf16[2,16,2048]{2,1,0:T(8,128)(2,1)}, bf16[2,16,2048]{2,1,0:T(8,128)(2,1)S(1)}, u32[]{:S(2)}, u32[]{:S(2)}) collective-permute-start(bf16[2,16,2048]{2,1,0:T(8,128)(2,1)} %get-tuple-element.768), channel_id=1, source_target_pairs={{32,0},{64,32},{96,64},{128,96},{160,128},{192,160},{224,192},{256... | collective-permute-start | bytes 393224 | tf_op jit(solution)/shard_map/while/body/eval_jaxpr/ppermute | solution.py:21
  615.3 1.3 collective-permute-start
  617.4 3.7 collective-permute-done
  622.6 4.0 collective-permute-start.1
  629.6 40.4 %collective-permute-done = bf16[2,16,2048]{2,1,0:T(8,128)(2,1)S(1)} collective-permute-done((bf16[2,16,2048]{2,1,0:T(8,128)(2,1)S(1)}, bf16[2,16,2048]{2,1,0:T(8,128)(2,1)S(1)}, u32[]{:S(2)}, u32[]{:S(2)}) %collective-permute-start) | collective-permute-done | bytes 131104 | tf_op jit(solution)/shard_map/while/body/eval_jaxpr/ppermute | solution.py:21
  671.6 5.5 collective-permute-start.1
  680.1 3.7 collective-permute-done
  685.3 36.6 %collective-permute-start.1 = (bf16[2,16,2048]{2,1,0:T(8,128)(2,1)}, bf16[2,16,2048]{2,1,0:T(8,128)(2,1)S(1)}, u32[]{:S(2)}, u32[]{:S(2)}) collective-permute-start(bf16[2,16,2048]{2,1,0:T(8,128)(2,1)} %get-tuple-element.768), channel_id=1, source_target_pairs={{32,0},{64,32},{96,64},{128,96},{160,128},{192,160},{224,192},{256... | collective-permute-start | bytes 393224 | tf_op jit(solution)/shard_map/while/body/eval_jaxpr/ppermute | solution.py:21
  724.9 3.7 collective-permute-done
  730.1 5.5 collective-permute-start.1
  738.6 36.9 %collective-permute-done = bf16[2,16,2048]{2,1,0:T(8,128)(2,1)S(1)} collective-permute-done((bf16[2,16,2048]{2,1,0:T(8,128)(2,1)S(1)}, bf16[2,16,2048]{2,1,0:T(8,128)(2,1)S(1)}, u32[]{:S(2)}, u32[]{:S(2)}) %collective-permute-start) | collective-permute-done | bytes 131104 | tf_op jit(solution)/shard_map/while/body/eval_jaxpr/ppermute | solution.py:21
  777.0 5.5 collective-permute-start.1
  785.5 3.7 collective-permute-done
  790.7 56.9 %collective-permute-start.1 = (bf16[2,16,2048]{2,1,0:T(8,128)(2,1)}, bf16[2,16,2048]{2,1,0:T(8,128)(2,1)S(1)}, u32[]{:S(2)}, u32[]{:S(2)}) collective-permute-start(bf16[2,16,2048]{2,1,0:T(8,128)(2,1)} %get-tuple-element.768), channel_id=1, source_target_pairs={{32,0},{64,32},{96,64},{128,96},{160,128},{192,160},{224,192},{256... | collective-permute-start | bytes 393224 | tf_op jit(solution)/shard_map/while/body/eval_jaxpr/ppermute | solution.py:21
  850.6 4.6 collective-permute-done
  856.7 45.0 %collective-permute-start.1 = (bf16[2,16,2048]{2,1,0:T(8,128)(2,1)}, bf16[2,16,2048]{2,1,0:T(8,128)(2,1)S(1)}, u32[]{:S(2)}, u32[]{:S(2)}) collective-permute-start(bf16[2,16,2048]{2,1,0:T(8,128)(2,1)} %get-tuple-element.768), channel_id=1, source_target_pairs={{32,0},{64,32},{96,64},{128,96},{160,128},{192,160},{224,192},{256... | collective-permute-start | bytes 393224 | tf_op jit(solution)/shard_map/while/body/eval_jaxpr/ppermute | solution.py:21
  904.7 43.2 %collective-permute-done = bf16[2,16,2048]{2,1,0:T(8,128)(2,1)S(1)} collective-permute-done((bf16[2,16,2048]{2,1,0:T(8,128)(2,1)S(1)}, bf16[2,16,2048]{2,1,0:T(8,128)(2,1)S(1)}, u32[]{:S(2)}, u32[]{:S(2)}) %collective-permute-start) | collective-permute-done | bytes 131104 | tf_op jit(solution)/shard_map/while/body/eval_jaxpr/ppermute | solution.py:21
  949.4 42.9 %collective-permute-start.1 = (bf16[2,16,2048]{2,1,0:T(8,128)(2,1)}, bf16[2,16,2048]{2,1,0:T(8,128)(2,1)S(1)}, u32[]{:S(2)}, u32[]{:S(2)}) collective-permute-start(bf16[2,16,2048]{2,1,0:T(8,128)(2,1)} %get-tuple-element.768), channel_id=1, source_target_pairs={{32,0},{64,32},{96,64},{128,96},{160,128},{192,160},{224,192},{256... | collective-permute-start | bytes 393224 | tf_op jit(solution)/shard_map/while/body/eval_jaxpr/ppermute | solution.py:21
  995.4 43.2 %collective-permute-done = bf16[2,16,2048]{2,1,0:T(8,128)(2,1)S(1)} collective-permute-done((bf16[2,16,2048]{2,1,0:T(8,128)(2,1)S(1)}, bf16[2,16,2048]{2,1,0:T(8,128)(2,1)S(1)}, u32[]{:S(2)}, u32[]{:S(2)}) %collective-permute-start) | collective-permute-done | bytes 131104 | tf_op jit(solution)/shard_map/while/body/eval_jaxpr/ppermute | solution.py:21
  1040.1 45.0 %collective-permute-start.1 = (bf16[2,16,2048]{2,1,0:T(8,128)(2,1)}, bf16[2,16,2048]{2,1,0:T(8,128)(2,1)S(1)}, u32[]{:S(2)}, u32[]{:S(2)}) collective-permute-start(bf16[2,16,2048]{2,1,0:T(8,128)(2,1)} %get-tuple-element.768), channel_id=1, source_target_pairs={{32,0},{64,32},{96,64},{128,96},{160,128},{192,160},{224,192},{256... | collective-permute-start | bytes 393224 | tf_op jit(solution)/shard_map/while/body/eval_jaxpr/ppermute | solution.py:21
  1088.1 43.2 %collective-permute-done = bf16[2,16,2048]{2,1,0:T(8,128)(2,1)S(1)} collective-permute-done((bf16[2,16,2048]{2,1,0:T(8,128)(2,1)S(1)}, bf16[2,16,2048]{2,1,0:T(8,128)(2,1)S(1)}, u32[]{:S(2)}, u32[]{:S(2)}) %collective-permute-start) | collective-permute-done | bytes 131104 | tf_op jit(solution)/shard_map/while/body/eval_jaxpr/ppermute | solution.py:21
  1132.9 42.9 %collective-permute-start.1 = (bf16[2,16,2048]{2,1,0:T(8,128)(2,1)}, bf16[2,16,2048]{2,1,0:T(8,128)(2,1)S(1)}, u32[]{:S(2)}, u32[]{:S(2)}) collective-permute-start(bf16[2,16,2048]{2,1,0:T(8,128)(2,1)} %get-tuple-element.768), channel_id=1, source_target_pairs={{32,0},{64,32},{96,64},{128,96},{160,128},{192,160},{224,192},{256... | collective-permute-start | bytes 393224 | tf_op jit(solution)/shard_map/while/body/eval_jaxpr/ppermute | solution.py:21
  1178.8 3.7 collective-permute-done
  1182.5 40.3 %conditional.10 = (f32[2,16,2048]{2,1,0:T(8,128)}, f32[1,2,16,2048]{3,2,1,0:T(8,128)S(1)}) conditional(s32[]{:T(128)} %convert_element_type.215, () %tuple.104, (pred[]{:T(512)}, f32[1,2,16,2048]{3,2,1,0:T(8,128)S(1)}, f32[2,16,2048]{2,1,0:T(8,128)S(1)}, bf16[2048,2048]{1,0:T(8,128)(2,1)}, s32[16]{0:T(128)}, ...), branch_computations={%region_1.1_spmd, %region_2.3_spmd} | conditional | flops 1311639808 | bytes 59262640 | solution.py:144
  1188.1 4.9 convolution_add_fusion.3
  1197.4 4.9 convolution_add_fusion.2
  1206.7 4.9 convolution_add_fusion.1
  1216.1 4.9 convolution_add_fusion
  1227.5 110.5 %psum.7 = f32[1,16]{1,0:T(1,128)} all-reduce(f32[1,16]{1,0:T(1,128)S(1)} %multiply_bitcast_fusion), channel_id=1, replica_groups=mesh['slot'=16,'row'=32] {'row'}, use_global_device_ids=true, to_apply=%region_8.10 | all-reduce | flops 16 | bytes 128 | tf_op jit(solution)/shard_map/psum | solution.py:175
  (313 shorter events, 138.1 us)
Async XLA Ops:
  8.9 25.1 %copy-start.4 = (s32[16,2]{0,1:T(2,128)S(1)}, s32[16,2]{0,1:T(2,128)}, u32[]{:S(2)}) copy-start(s32[16,2]{0,1:T(2,128)} %param.16) | copy-start | bytes 388
  8.9 386.7 %all-to-all-start = ((bf16[512,4,2048]{2,1,0:T(4,128)(2,1)}), bf16[512,4,2048]{2,1,0:T(4,128)(2,1)}, u32[]{:S(2)}, u32[]{:S(2)}) async-start(bf16[512,4,2048]{2,1,0:T(4,128)(2,1)} %stack.20), calls=%async_computation | async-start | bytes 16777216 | tf_op jit(solution)/shard_map/all_to_all | solution.py:8
  36.3 372.5 %copy-start = (bf16[16,128,128]{2,1,0:T(8,128)(2,1)S(1)}, bf16[16,128,128]{2,1,0:T(8,128)(2,1)}, u32[]{:S(2)}) copy-start(bf16[16,128,128]{2,1,0:T(8,128)(2,1)} %param.15) | copy-start | bytes 1572868
  36.3 372.5 %copy-start.1 = (f32[2,16,2048]{2,1,0:T(8,128)S(1)}, f32[2,16,2048]{2,1,0:T(8,128)}, u32[]{:S(2)}) copy-start(f32[2,16,2048]{2,1,0:T(8,128)} %param.18) | copy-start | bytes 786436
  36.3 372.5 %copy-start.3 = (f32[2,16,2048]{2,1,0:T(8,128)S(1)}, f32[2,16,2048]{2,1,0:T(8,128)}, u32[]{:S(2)}) copy-start(f32[2,16,2048]{2,1,0:T(8,128)} %param.19) | copy-start | bytes 786436
  408.9 817.7 %copy-start.5 = (pred[16]{0:T(512)(128)(4,1)S(1)}, pred[16]{0:T(512)(128)(4,1)}, u32[]{:S(2)}) copy-start(pred[16]{0:T(512)(128)(4,1)} %get-tuple-element.588) | copy-start | bytes 52
  408.9 817.7 %copy-start.6 = (pred[16]{0:T(512)(128)(4,1)S(1)}, pred[16]{0:T(512)(128)(4,1)}, u32[]{:S(2)}) copy-start(pred[16]{0:T(512)(128)(4,1)} %get-tuple-element.620) | copy-start | bytes 52
  409.1 5.2 collective-permute-start.1
  412.3 6.8 collective-permute-start
  459.3 4.2 collective-permute-start.1
  461.5 5.7 collective-permute-start
  468.8 43.1 %collective-permute-start.1 = (bf16[2,16,2048]{2,1,0:T(8,128)(2,1)}, bf16[2,16,2048]{2,1,0:T(8,128)(2,1)S(1)}, u32[]{:S(2)}, u32[]{:S(2)}) collective-permute-start(bf16[2,16,2048]{2,1,0:T(8,128)(2,1)} %get-tuple-element.768), channel_id=1, source_target_pairs={{32,0},{64,32},{96,64},{128,96},{160,128},{192,160},{224,192},{256... | collective-permute-start | bytes 393224 | tf_op jit(solution)/shard_map/while/body/eval_jaxpr/ppermute | solution.py:21
  509.9 5.7 collective-permute-start
  517.1 4.9 collective-permute-start.1
  520.0 42.5 %collective-permute-start = (bf16[2,16,2048]{2,1,0:T(8,128)(2,1)S(1)}, bf16[2,16,2048]{2,1,0:T(8,128)(2,1)S(1)}, u32[]{:S(2)}, u32[]{:S(2)}) collective-permute-start(bf16[2,16,2048]{2,1,0:T(8,128)(2,1)S(1)} %convert_element_type.216), channel_id=1, source_target_pairs={{0,32},{32,64},{64,96},{96,128},{128,160},{160,192},{192,224},{224... | collective-permute-start | bytes 393224 | tf_op jit(solution)/shard_map/while/body/eval_jaxpr/ppermute | solution.py:21
  564.1 6.3 collective-permute-start.1
  568.4 5.7 collective-permute-start
  575.6 41.6 %collective-permute-start.1 = (bf16[2,16,2048]{2,1,0:T(8,128)(2,1)}, bf16[2,16,2048]{2,1,0:T(8,128)(2,1)S(1)}, u32[]{:S(2)}, u32[]{:S(2)}) collective-permute-start(bf16[2,16,2048]{2,1,0:T(8,128)(2,1)} %get-tuple-element.768), channel_id=1, source_target_pairs={{32,0},{64,32},{96,64},{128,96},{160,128},{192,160},{224,192},{256... | collective-permute-start | bytes 393224 | tf_op jit(solution)/shard_map/while/body/eval_jaxpr/ppermute | solution.py:21
  615.3 5.7 collective-permute-start
  622.6 7.0 collective-permute-start.1
  627.6 42.5 %collective-permute-start = (bf16[2,16,2048]{2,1,0:T(8,128)(2,1)S(1)}, bf16[2,16,2048]{2,1,0:T(8,128)(2,1)S(1)}, u32[]{:S(2)}, u32[]{:S(2)}) collective-permute-start(bf16[2,16,2048]{2,1,0:T(8,128)(2,1)S(1)} %convert_element_type.216), channel_id=1, source_target_pairs={{0,32},{32,64},{64,96},{96,128},{128,160},{160,192},{192,224},{224... | collective-permute-start | bytes 393224 | tf_op jit(solution)/shard_map/while/body/eval_jaxpr/ppermute | solution.py:21
  671.6 8.4 collective-permute-start.1
  678.0 5.7 collective-permute-start
  685.3 39.5 %collective-permute-start.1 = (bf16[2,16,2048]{2,1,0:T(8,128)(2,1)}, bf16[2,16,2048]{2,1,0:T(8,128)(2,1)S(1)}, u32[]{:S(2)}, u32[]{:S(2)}) collective-permute-start(bf16[2,16,2048]{2,1,0:T(8,128)(2,1)} %get-tuple-element.768), channel_id=1, source_target_pairs={{32,0},{64,32},{96,64},{128,96},{160,128},{192,160},{224,192},{256... | collective-permute-start | bytes 393224 | tf_op jit(solution)/shard_map/while/body/eval_jaxpr/ppermute | solution.py:21
  722.8 5.7 collective-permute-start
  730.1 8.4 collective-permute-start.1
  736.5 38.9 %collective-permute-start = (bf16[2,16,2048]{2,1,0:T(8,128)(2,1)S(1)}, bf16[2,16,2048]{2,1,0:T(8,128)(2,1)S(1)}, u32[]{:S(2)}, u32[]{:S(2)}) collective-permute-start(bf16[2,16,2048]{2,1,0:T(8,128)(2,1)S(1)} %convert_element_type.216), channel_id=1, source_target_pairs={{0,32},{32,64},{64,96},{96,128},{128,160},{160,192},{192,224},{224... | collective-permute-start | bytes 393224 | tf_op jit(solution)/shard_map/while/body/eval_jaxpr/ppermute | solution.py:21
  777.0 8.4 collective-permute-start.1
  783.4 5.7 collective-permute-start
  790.7 59.8 %collective-permute-start.1 = (bf16[2,16,2048]{2,1,0:T(8,128)(2,1)}, bf16[2,16,2048]{2,1,0:T(8,128)(2,1)S(1)}, u32[]{:S(2)}, u32[]{:S(2)}) collective-permute-start(bf16[2,16,2048]{2,1,0:T(8,128)(2,1)} %get-tuple-element.768), channel_id=1, source_target_pairs={{32,0},{64,32},{96,64},{128,96},{160,128},{192,160},{224,192},{256... | collective-permute-start | bytes 393224 | tf_op jit(solution)/shard_map/while/body/eval_jaxpr/ppermute | solution.py:21
  848.5 6.6 collective-permute-start
  856.7 47.9 %collective-permute-start.1 = (bf16[2,16,2048]{2,1,0:T(8,128)(2,1)}, bf16[2,16,2048]{2,1,0:T(8,128)(2,1)S(1)}, u32[]{:S(2)}, u32[]{:S(2)}) collective-permute-start(bf16[2,16,2048]{2,1,0:T(8,128)(2,1)} %get-tuple-element.768), channel_id=1, source_target_pairs={{32,0},{64,32},{96,64},{128,96},{160,128},{192,160},{224,192},{256... | collective-permute-start | bytes 393224 | tf_op jit(solution)/shard_map/while/body/eval_jaxpr/ppermute | solution.py:21
  902.7 45.2 %collective-permute-start = (bf16[2,16,2048]{2,1,0:T(8,128)(2,1)S(1)}, bf16[2,16,2048]{2,1,0:T(8,128)(2,1)S(1)}, u32[]{:S(2)}, u32[]{:S(2)}) collective-permute-start(bf16[2,16,2048]{2,1,0:T(8,128)(2,1)S(1)} %convert_element_type.216), channel_id=1, source_target_pairs={{0,32},{32,64},{64,96},{96,128},{128,160},{160,192},{192,224},{224... | collective-permute-start | bytes 393224 | tf_op jit(solution)/shard_map/while/body/eval_jaxpr/ppermute | solution.py:21
  949.4 45.8 %collective-permute-start.1 = (bf16[2,16,2048]{2,1,0:T(8,128)(2,1)}, bf16[2,16,2048]{2,1,0:T(8,128)(2,1)S(1)}, u32[]{:S(2)}, u32[]{:S(2)}) collective-permute-start(bf16[2,16,2048]{2,1,0:T(8,128)(2,1)} %get-tuple-element.768), channel_id=1, source_target_pairs={{32,0},{64,32},{96,64},{128,96},{160,128},{192,160},{224,192},{256... | collective-permute-start | bytes 393224 | tf_op jit(solution)/shard_map/while/body/eval_jaxpr/ppermute | solution.py:21
  993.3 45.2 %collective-permute-start = (bf16[2,16,2048]{2,1,0:T(8,128)(2,1)S(1)}, bf16[2,16,2048]{2,1,0:T(8,128)(2,1)S(1)}, u32[]{:S(2)}, u32[]{:S(2)}) collective-permute-start(bf16[2,16,2048]{2,1,0:T(8,128)(2,1)S(1)} %convert_element_type.216), channel_id=1, source_target_pairs={{0,32},{32,64},{64,96},{96,128},{128,160},{160,192},{192,224},{224... | collective-permute-start | bytes 393224 | tf_op jit(solution)/shard_map/while/body/eval_jaxpr/ppermute | solution.py:21
  1040.1 47.9 %collective-permute-start.1 = (bf16[2,16,2048]{2,1,0:T(8,128)(2,1)}, bf16[2,16,2048]{2,1,0:T(8,128)(2,1)S(1)}, u32[]{:S(2)}, u32[]{:S(2)}) collective-permute-start(bf16[2,16,2048]{2,1,0:T(8,128)(2,1)} %get-tuple-element.768), channel_id=1, source_target_pairs={{32,0},{64,32},{96,64},{128,96},{160,128},{192,160},{224,192},{256... | collective-permute-start | bytes 393224 | tf_op jit(solution)/shard_map/while/body/eval_jaxpr/ppermute | solution.py:21
  1086.1 45.2 %collective-permute-start = (bf16[2,16,2048]{2,1,0:T(8,128)(2,1)S(1)}, bf16[2,16,2048]{2,1,0:T(8,128)(2,1)S(1)}, u32[]{:S(2)}, u32[]{:S(2)}) collective-permute-start(bf16[2,16,2048]{2,1,0:T(8,128)(2,1)S(1)} %convert_element_type.216), channel_id=1, source_target_pairs={{0,32},{32,64},{64,96},{96,128},{128,160},{160,192},{192,224},{224... | collective-permute-start | bytes 393224 | tf_op jit(solution)/shard_map/while/body/eval_jaxpr/ppermute | solution.py:21
  1132.9 45.8 %collective-permute-start.1 = (bf16[2,16,2048]{2,1,0:T(8,128)(2,1)}, bf16[2,16,2048]{2,1,0:T(8,128)(2,1)S(1)}, u32[]{:S(2)}, u32[]{:S(2)}) collective-permute-start(bf16[2,16,2048]{2,1,0:T(8,128)(2,1)} %get-tuple-element.768), channel_id=1, source_target_pairs={{32,0},{64,32},{96,64},{128,96},{160,128},{192,160},{224,192},{256... | collective-permute-start | bytes 393224 | tf_op jit(solution)/shard_map/while/body/eval_jaxpr/ppermute | solution.py:21
  1176.7 5.7 collective-permute-start
  1223.5 114.5 %copy-start.2 = (f32[1,2,16,2048]{3,2,1,0:T(8,128)}, f32[1,2,16,2048]{3,2,1,0:T(8,128)S(1)}, u32[]{:S(2)}) copy-start(f32[1,2,16,2048]{3,2,1,0:T(8,128)S(1)} %get-tuple-element.394) | copy-start | bytes 786436
